TPU v7x, 512 devices: a whole 4x8x8 slice. The times are simulated.
512 devices in a mesh: gx: 8 (over z), gy: 8 (over y_lo, core), gz: 8 (over y_hi, x).
Axes of the slice: x: 4, y: 8 (y_hi: 2, y_lo: 4; y = y_hi * 4 + y_lo), z: 8, core: 2. Of those that a mesh axis runs over, the one named last changes fastest.
Arguments:
- x_in: bfloat16 [3072, 5120], P(('gy', 'gx'), 'gz'), may hold values from -190 to 190
- gain: float32 [5120], P('gz'), may hold values from 0.25 to 1.75
- w_up: bfloat16 [5120, 7168], P(('gz', 'gy'), 'gx'), may hold values from -0.078125 to 0.078125
- w_down: bfloat16 [7168, 5120], P(('gx', 'gy'), 'gz'), may hold values from -0.0625 to 0.0625
- d_out: bfloat16 [3072, 5120], P(('gy', 'gx'), 'gz'), may hold values from -1.1953125 to 1.1953125
Outputs:
- d_x: bfloat16 [3072, 5120], P(('gy', 'gx'), 'gz')
- d_w_up: bfloat16 [5120, 7168], P(('gz', 'gy'), 'gx')
- d_w_down: bfloat16 [7168, 5120], P(('gx', 'gy'), 'gz')
- d_gain: float32 [5120], P('gz')
All inputs are finite; a program needn't handle non-finite values.
Results may differ from a plain program's by a relative error of at most 0.02.
Values may be sent and summed in bfloat16 or wider, within the bound.
No kernel may reach another device: no remote copies, remote signals or barrier semaphores. Data moves between devices by JAX's collectives and lax.ppermute only.
A program may use at most 64 MiB of HBM per device.

v0:
```python
import jax
import jax.numpy as jnp
from jax import lax
from jax.sharding import Mesh
from jax.sharding import PartitionSpec as P

BF, F32 = (jnp.bfloat16, jnp.float32)
LANES = 128
GY, GZ = (("yl", "co"), ("yh", "xx"))


def gelu_pair(hidden):
    cdf = 0.5 * (1.0 + jax.scipy.special.erf(hidden * 0.7071067811865476))
    slope = cdf + hidden * jnp.exp(-0.5 * hidden * hidden) * 0.3989422804014327
    return (hidden * cdf, slope)


def exchange(blocks, axis):
    return lax.all_to_all(blocks, axis, 0, 0, tiled=True)


def spread(value, axis):
    n = lax.axis_size(axis)
    return exchange(jnp.broadcast_to(value[None], (n, *value.shape)), axis)


def summed(blocks):
    return jnp.sum(blocks.astype(F32), axis=0)


def pieces(value):
    high = lax.reduce_precision(value, 8, 7)
    rest = value - high
    middle = lax.reduce_precision(rest, 8, 7)
    return [p.astype(BF) for p in (high, middle, rest - middle)]


def columns(*values):
    return jnp.stack([p for v in values for p in pieces(v)], axis=-1)


def column(lanes, index):
    return jnp.sum(lanes[..., 3 * index : 3 * index + 3].astype(F32), axis=-1)


def swap(value, axis, bits):
    return lax.ppermute(value, axis, [(i, i ^ bits) for i in range(lax.axis_size(axis))])


def other_core(value):
    return swap(value, "co", 1)


def dot(a, b, contract):
    return lax.dot_general(
        a, b, ((contract[:1], contract[1:]), ((), ())), preferred_element_type=F32
    )


def body(x_in, gain, w_up, w_down, d_out):
    rows, local = x_in.shape
    n_gx, n_yl, n_gz = (lax.axis_size(a) for a in ("gx", "yl", GZ))
    width = local * n_gz
    up_rows, hid = w_up.shape
    down_rows = w_down.shape[0]
    all_rows = rows * n_gx
    block = all_rows // n_gz
    even = lax.axis_index("co") == 0

    def by_core(mine, other):
        pair = [jnp.where(even, mine, other), jnp.where(even, other, mine)]
        return jnp.stack(pair, axis=1).reshape(-1, mine.shape[-1])

    down_full = lax.all_gather(w_down, GY, axis=0, tiled=True)
    up_mine = spread(w_up, "yl")
    both = lax.all_gather(jnp.concatenate([x_in, d_out], axis=1), "gx", axis=0, tiled=True)
    both, up_mine = lax.optimization_barrier((both, up_mine))
    up_full = by_core(up_mine, other_core(up_mine))
    x_rows, out_rows = (both[:, :local].astype(F32), both[:, local:])
    part_sum = jnp.sum(x_rows, axis=1)
    off = x_rows - (part_sum / local)[:, None]
    second = jnp.sum(off * off, axis=1)
    y = (off * gain).astype(BF)
    gains = jnp.pad(jnp.stack(pieces(gain)), ((0, 5), (0, 0)))
    tilt = jnp.sum(dot(gains, up_full, (1, 0)), axis=0)
    tilt = jnp.stack(pieces(tilt)).reshape(3 * n_gz, -1)
    spare = LANES - tilt.shape[1]
    tilt = jnp.pad(tilt, ((0, block - tilt.shape[0]), (0, 0)))
    marks = columns(part_sum, second)
    extra = jnp.concatenate(
        [
            jnp.pad(marks, ((0, 0), (0, spare - marks.shape[1]))).reshape(n_gz, block, spare),
            jnp.broadcast_to(tilt, (n_gz, *tilt.shape)),
        ],
        axis=2,
    )
    pair = jnp.concatenate(
        [
            dot(y, up_full, (1, 0)).astype(BF).reshape(n_gz, block, hid),
            dot(out_rows, down_full, (1, 1)).astype(BF).reshape(n_gz, block, hid),
            extra,
        ],
        axis=2,
    )
    pair = exchange(pair, GZ)
    marks = pair[:, :, 2 * hid : 2 * hid + spare]
    tilts = pair[:, : 3 * n_gz, 2 * hid + spare :].astype(F32)
    tilts = jnp.sum(tilts.reshape(n_gz, 3, n_gz, -1), axis=1).reshape(n_gz, hid)
    means = column(marks, 0) / local
    mean = jnp.sum(means, axis=0) / n_gz
    shift = means - mean
    var = (jnp.sum(column(marks, 1), axis=0) + local * jnp.sum(shift * shift, axis=0)) / width
    inv = lax.rsqrt(var + 1e-05)
    hidden = summed(pair[:, :, :hid]) + sum(
        (shift[i][:, None] * tilts[i][None] for i in range(n_gz))
    )
    hidden = hidden * inv[:, None]
    d_act = summed(pair[:, :, hid : 2 * hid])
    act_f, slope = gelu_pair(hidden)
    d_hidden = (d_act * slope).astype(BF)
    cross = jnp.sum(d_hidden.astype(F32) * hidden, axis=1)
    marks = columns(cross, mean, inv)
    marks = jnp.pad(marks, ((0, 0), (0, LANES - marks.shape[1])))
    acts = jnp.concatenate([act_f.astype(BF), d_hidden, marks], axis=1)
    acts = spread(acts, GZ).reshape(all_rows, -1)
    act_rows, hgrad_rows, marks = (acts[:, :hid], acts[:, hid : 2 * hid], acts[:, 2 * hid :])
    cross, mean, inv = (column(marks, i) for i in range(3))
    normed = (x_rows - mean[:, None]) * inv[:, None]
    z = (normed * gain).astype(BF)
    dz_part = dot(hgrad_rows, up_full, (1, 1))
    level = jnp.sum(hgrad_rows.astype(F32) * jnp.sum(tilts, axis=0), axis=1)
    marks = columns(level, cross)
    tail = jnp.concatenate(
        [dz_part.astype(BF), jnp.pad(marks, ((0, 0), (0, LANES - marks.shape[1])))], axis=1
    ).reshape(n_gx, rows, local + LANES)
    gain_part = jnp.stack(pieces(jnp.sum(dz_part * normed, axis=0)))
    gain_part = jnp.pad(gain_part, ((0, 5), (0, LANES)))
    tail = jnp.concatenate([tail, jnp.broadcast_to(gain_part, (n_gx, *gain_part.shape))], axis=1)
    tail, acts = lax.optimization_barrier((tail, acts))
    act_rows, hgrad_rows = (acts[:, :hid], acts[:, hid : 2 * hid])
    tail = exchange(tail, "gx")

    def chunks(value, height):
        cut = [value[:, i : i + LANES] for i in range(0, value.shape[1], LANES)]
        return [c.reshape(n_yl, 2, height, LANES) for c in cut]

    grads = jnp.concatenate(
        [
            *chunks(dot(act_rows, out_rows, (0, 0)).astype(BF), down_rows),
            *chunks(dot(z, hgrad_rows, (0, 0)).astype(BF), up_rows),
        ],
        axis=2,
    )
    keep = jnp.where(even, grads[:, 0], grads[:, 1])
    give = jnp.where(even, grads[:, 1], grads[:, 0])
    grads = (keep.astype(F32) + other_core(give).astype(F32)).astype(BF)
    place = lax.axis_index("yl")

    def part(index):
        return lax.dynamic_index_in_dim(grads, index, keepdims=False)

    grads = [part(place)] + [swap(part(place ^ k), "yl", k) for k in range(1, n_yl)]
    d_z = summed(tail[:, :rows, :local])
    marks = summed(tail[:, :rows, local:])
    scaled_sum, cross_sum = (column(marks, i)[:, None] / width for i in range(2))
    d_gain = jnp.sum(tail[:, rows : rows + 3, :local].astype(F32), axis=(0, 1))
    for axis, bits in (("yl", 1), ("yl", 2), ("co", 1)):
        d_gain = d_gain + swap(d_gain, axis, bits)

    def unchunk(first, height, count):
        cut = [slice(first + i * height, first + (i + 1) * height) for i in range(count)]
        cut = [sum((g[c].astype(F32) for g in grads)) for c in cut]
        return jnp.concatenate([c.astype(BF) for c in cut], axis=1)

    d_w_down = unchunk(0, down_rows, local // LANES)
    d_w_up = unchunk(down_rows * (local // LANES), up_rows, hid // LANES)
    first = lax.axis_index("gx") * rows

    def own(values):
        return lax.dynamic_slice(values, (first,), (rows,))[:, None]

    own_inv = own(inv)
    own_normed = (x_in.astype(F32) - own(mean)) * own_inv
    d_x = own_inv * (d_z * gain - scaled_sum - own_normed * cross_sum)
    return (d_x.astype(BF), d_w_up, d_w_down, d_gain)


def solution(mesh):
    sizes = mesh.shape
    cores, x_chips = (2, sizes["gz"] // 2)
    fine = Mesh(
        mesh.devices.reshape(sizes["gx"], sizes["gy"] // cores, cores, 2, x_chips), ("gx", *GY, *GZ)
    )
    placed = (
        P((*GY, "gx"), GZ),
        P(GZ),
        P((*GZ, *GY), "gx"),
        P(("gx", *GY), GZ),
        P((*GY, "gx"), GZ),
    )
    return jax.shard_map(
        body,
        mesh=fine,
        in_specs=placed,
        out_specs=(P((*GY, "gx"), GZ), P((*GZ, *GY), "gx"), P(("gx", *GY), GZ), P(GZ)),
        check_vma=False,
    )
```

profile of v0, /device:TPU:1, one launch (start us, length us, event | category | flops | bytes accessed | tf_op | source)
XLA Modules:
  0.0 213.0 jit_solution(7166205176979230896)
XLA Ops:
  7.2 0.7 all-gather.2.cloned.1.call-update
  7.9 1.8 broadcast_in_dim.8
  9.7 5.4 %all-to-all-start = ((bf16[4,80,896]{2,1,0:T(8,128)(2,1)}), bf16[4,80,896]{2,1,0:T(8,128)(2,1)S(1)}, u32[]{:S(2)}, u32[]{:S(2)}) async-start(bf16[4,80,896]{2,1,0:T(8,128)(2,1)} %broadcast_in_dim.8), calls=%async_computation | async-start | bytes 1146880 | tf_op jit(solution)/shard_map/all_to_all | solution.py:19
  15.2 28.2 %all_gather.6 = bf16[384,1280]{1,0:T(8,128)(2,1)S(1)} all-gather(bf16[48,1280]{1,0:T(8,128)(2,1)S(1)} %pad_maximum_fusion.2), channel_id=1, replica_groups=mesh['gx'=8,'yl'=4,'co'=2,'yh'=2,'xx'=4] {'gx'}, dimensions={0}, use_global_device_ids=true | all-gather | bytes 1105920 | tf_op jit(solution)/shard_map/all_gather | solution.py:76
  43.4 7.5 %collective-permute-start = (bf16[4,80,896]{2,1,0:T(8,128)(2,1)S(1)}, bf16[4,80,896]{2,1,0:T(8,128)(2,1)S(1)}, u32[]{:S(2)}, u32[]{:S(2)}) collective-permute-start(bf16[4,80,896]{2,1,0:T(8,128)(2,1)S(1)} %all-to-all-done), channel_id=1, source_target_pairs={{0,8},{8,0},{1,9},{9,1},{2,10},{10,2},{3,11},{11,3},{4,12},{12,4},... | collective-permute-start | bytes 1720328 | tf_op jit(solution)/shard_map/ppermute | solution.py:47
  51.0 0.1 convert_reduce_fusion
  51.1 0.3 fusion.5
  51.5 0.2 copy.145
  51.7 0.9 collective-permute-done
  52.6 0.1 select_bitcast_fusion.2
  52.7 0.1 pad_maximum_fusion
  52.8 0.3 convolution_reduce_fusion
  53.1 0.1 reshape.504
  53.2 1.7 convolution_convert_fusion.3
  55.0 2.9 %convolution_convert_fusion.2 = bf16[384,896]{1,0:T(8,128)(2,1)} fusion(bf16[896,640]{1,0:T(8,128)(2,1)} %all-gather.2.cloned.1.call-done, bf16[384,1280]{1,0:T(8,128)(2,1)S(1)} %all_gather.6), kind=kOutput, calls=%fused_computation.10 | convolution fusion | flops 440745984 | bytes 2326528 | tf_op jit(solution)/shard_map/dot_general | solution.py:55
  57.9 2.1 %concatenate.25 = bf16[8,48,1920]{2,1,0:T(8,128)(2,1)S(1)} concatenate(bf16[8,48,896]{2,1,0:T(8,128)(2,1)S(1)} %bitcast.163, bf16[8,48,896]{2,1,0:T(8,128)(2,1)} %bitcast.164, bf16[8,48,16]{2,1,0:T(8,128)(2,1)S(1)} %bitcast.172, bf16[8,48,112]{2,1,0:T(8,128)(2,1)S(1)} %broadcast_in_dim.9), dimensions={2} | concatenate | bytes 2949120 | tf_op jit(solution)/shard_map/concatenate | solution.py:97
  60.1 31.1 %all_to_all.20 = bf16[8,48,1920]{2,1,0:T(8,128)(2,1)S(1)} all-to-all(bf16[8,48,1920]{2,1,0:T(8,128)(2,1)S(1)} %concatenate.25), channel_id=1, replica_groups=mesh['gx'=8,'yl'=4,'co'=2,'yh'=2,'xx'=4] {'yh','xx'}, dimensions={0} | all-to-all | bytes 2949120 | tf_op jit(solution)/shard_map/all_to_all | solution.py:19
  91.2 0.2 convert_reduce_fusion.6
  91.6 0.1 fusion.35
  91.9 0.1 mul.312
  92.0 0.1 mul.307
  92.0 0.1 mul.302
  92.1 0.1 mul.297
  92.2 0.1 mul.292
  92.3 0.2 convert_reduce_fusion.1
  92.5 0.2 multiply_convert_fusion
  92.7 0.2 multiply_reduce_fusion.1
  92.9 0.1 copy.146
  93.1 1.2 broadcast_in_dim.10
  94.3 4.3 %all-to-all-start.2 = ((bf16[8,48,1920]{2,1,0:T(8,128)(2,1)}), bf16[8,48,1920]{2,1,0:T(8,128)(2,1)}, u32[]{:S(2)}, u32[]{:S(2)}) async-start(bf16[8,48,1920]{2,1,0:T(8,128)(2,1)} %broadcast_in_dim.10), calls=%async_computation.2 | async-start | bytes 2949120 | tf_op jit(solution)/shard_map/all_to_all | solution.py:19
  98.6 0.1 convert_reduce_fusion.7
  98.8 15.7 %all-to-all-done.2 = bf16[8,48,1920]{2,1,0:T(8,128)(2,1)} async-done(((bf16[8,48,1920]{2,1,0:T(8,128)(2,1)}), bf16[8,48,1920]{2,1,0:T(8,128)(2,1)}, u32[]{:S(2)}, u32[]{:S(2)}) %all-to-all-start.2) | async-done | bytes 1474592 | tf_op jit(solution)/shard_map/all_to_all | solution.py:19
  114.4 1.2 fusion.108
  115.6 1.3 multiply_reduce_fusion
  117.0 0.1 copy.141
  117.1 0.1 copy.140
  117.2 0.1 copy.142
  117.4 2.1 fusion.111
  119.5 0.2 copy.120
  119.8 0.9 pad_maximum_fusion.1
  120.7 2.1 convolution_convert_fusion
  122.8 1.9 convolution_convert_fusion.1
  124.8 0.2 fusion.109
  125.0 0.2 fusion.110
  125.6 0.1 select_bitcast_fusion
  125.7 19.9 %collective-permute-start.1 = (bf16[4,1120,128]{2,1,0:T(8,128)(2,1)S(1)}, bf16[4,1120,128]{2,1,0:T(8,128)(2,1)}, u32[]{:S(2)}, u32[]{:S(2)}) collective-permute-start(bf16[4,1120,128]{2,1,0:T(8,128)(2,1)S(1)} %select_bitcast_fusion), channel_id=1, source_target_pairs={{0,8},{8,0},{1,9},{9,1},{2,10},{10,2},{3,11},{11,3},{4,12},{12,4},... | collective-permute-start | bytes 3440648 | tf_op jit(solution)/shard_map/ppermute | solution.py:47
  145.6 4.2 %all-to-all-start.3 = ((bf16[8,56,768]{2,1,0:T(8,128)(2,1)}), bf16[8,56,768]{2,1,0:T(8,128)(2,1)}, u32[]{:S(2)}, u32[]{:S(2)}) async-start(bf16[8,56,768]{2,1,0:T(8,128)(2,1)} %pad_maximum_fusion.1), calls=%async_computation.3 | async-start | bytes 1376256 | tf_op jit(solution)/shard_map/all_to_all | solution.py:19
  149.8 0.1 dynamic_slice.19
  150.0 1.7 fusion
  151.8 20.0 %collective-permute-start.2 = (bf16[1120,128]{1,0:T(8,128)(2,1)S(1)}, bf16[1120,128]{1,0:T(8,128)(2,1)S(1)}, u32[]{:S(2)}, u32[]{:S(2)}) collective-permute-start(bf16[1120,128]{1,0:T(8,128)(2,1)S(1)} %get-tuple-element.29), channel_id=1, source_target_pairs={{0,16},{16,0},{32,48},{48,32},{1,17},{17,1},{33,49},{49,33},{2,18}... | collective-permute-start | bytes 860168 | tf_op jit(solution)/shard_map/ppermute | solution.py:47
  171.8 2.0 collective-permute-start.4
  173.8 3.0 %collective-permute-start.3 = (bf16[1120,128]{1,0:T(8,128)(2,1)S(1)}, bf16[1120,128]{1,0:T(8,128)(2,1)S(1)}, u32[]{:S(2)}, u32[]{:S(2)}) collective-permute-start(bf16[1120,128]{1,0:T(8,128)(2,1)S(1)} %get-tuple-element.31), channel_id=1, source_target_pairs={{0,32},{16,48},{32,0},{48,16},{1,33},{17,49},{33,1},{49,17},{2,34}... | collective-permute-start | bytes 860168 | tf_op jit(solution)/shard_map/ppermute | solution.py:47
  176.8 0.9 convert_reduce_fusion.8
  177.7 14.6 %collective-permute-start.5 = (f32[640]{0:T(1024)S(1)}, f32[640]{0:T(1024)S(1)}, u32[]{:S(2)}, u32[]{:S(2)}) collective-permute-start(f32[640]{0:T(1024)S(1)} %convert_reduce_fusion.8), channel_id=1, source_target_pairs={{0,16},{16,0},{32,48},{48,32},{1,17},{17,1},{33,49},{49,33},{2,18}... | collective-permute-start | bytes 7688 | tf_op jit(solution)/shard_map/ppermute | solution.py:47
  192.3 0.9 convert_reduce_fusion.4
  193.2 0.2 slice_reduce_fusion.1
  193.5 2.5 %collective-permute-start.6 = (f32[640]{0:T(1024)S(1)}, f32[640]{0:T(1024)S(1)}, u32[]{:S(2)}, u32[]{:S(2)}) collective-permute-start(f32[640]{0:T(1024)S(1)} %add.288), channel_id=1, source_target_pairs={{0,32},{16,48},{32,0},{48,16},{1,33},{17,49},{33,1},{49,17},{2,34}... | collective-permute-start | bytes 7688 | tf_op jit(solution)/shard_map/ppermute | solution.py:47
  195.9 1.1 convert_reduce_fusion.3
  197.0 3.0 %collective-permute-done.6 = f32[640]{0:T(1024)S(1)} collective-permute-done((f32[640]{0:T(1024)S(1)}, f32[640]{0:T(1024)S(1)}, u32[]{:S(2)}, u32[]{:S(2)}) %collective-permute-start.6) | collective-permute-done | bytes 2592 | tf_op jit(solution)/shard_map/ppermute | solution.py:47
  200.1 3.0 %collective-permute-start.7 = (f32[640]{0:T(1024)S(1)}, f32[640]{0:T(1024)S(1)}, u32[]{:S(2)}, u32[]{:S(2)}) collective-permute-start(f32[640]{0:T(1024)S(1)} %add.289), channel_id=1, source_target_pairs={{0,8},{8,0},{1,9},{9,1},{2,10},{10,2},{3,11},{11,3},{4,12},{12,4},... | collective-permute-start | bytes 7688 | tf_op jit(solution)/shard_map/ppermute | solution.py:47
  203.1 0.7 multiply_convert_fusion.1
  203.9 0.6 add.290
  205.0 0.5 copy-done.9
  205.5 0.7 copy-done.8
  (97 shorter events, 1.9 us)
Async XLA Ops:
  7.2 8.0 %copy-start.7 = (f32[640]{0:T(1024)S(1)}, f32[640]{0:T(1024)}, u32[]{:S(2)}) copy-start(f32[640]{0:T(1024)} %param.6) | copy-start | bytes 7684
  7.2 8.0 %copy-start.5 = (bf16[48,640]{1,0:T(8,128)(2,1)S(1)}, bf16[48,640]{1,0:T(8,128)(2,1)}, u32[]{:S(2)}) copy-start(bf16[48,640]{1,0:T(8,128)(2,1)} %param.5) | copy-start | bytes 184324
  7.2 8.0 %copy-start.6 = (bf16[48,640]{1,0:T(8,128)(2,1)S(1)}, bf16[48,640]{1,0:T(8,128)(2,1)}, u32[]{:S(2)}) copy-start(bf16[48,640]{1,0:T(8,128)(2,1)} %param.9) | copy-start | bytes 184324
  7.2 47.8 %all-gather.2.cloned.1.call-start = ((), (), s32[]{:S(2)}) async-start(), calls=%async_computation.4 | async-start | bytes 1290240 | tf_op jit(solution)/shard_map/all_gather | solution.py:74
  9.7 33.7 %all-to-all-start = ((bf16[4,80,896]{2,1,0:T(8,128)(2,1)}), bf16[4,80,896]{2,1,0:T(8,128)(2,1)S(1)}, u32[]{:S(2)}, u32[]{:S(2)}) async-start(bf16[4,80,896]{2,1,0:T(8,128)(2,1)} %broadcast_in_dim.8), calls=%async_computation | async-start | bytes 1146880 | tf_op jit(solution)/shard_map/all_to_all | solution.py:19
  43.4 11.5 %copy-start.2 = (bf16[384,1280]{1,0:T(8,128)(2,1)}, bf16[384,1280]{1,0:T(8,128)(2,1)S(1)}, u32[]{:S(2)}) copy-start(bf16[384,1280]{1,0:T(8,128)(2,1)S(1)} %all_gather.6) | copy-start | bytes 2949124
  43.4 9.1 %collective-permute-start = (bf16[4,80,896]{2,1,0:T(8,128)(2,1)S(1)}, bf16[4,80,896]{2,1,0:T(8,128)(2,1)S(1)}, u32[]{:S(2)}, u32[]{:S(2)}) collective-permute-start(bf16[4,80,896]{2,1,0:T(8,128)(2,1)S(1)} %all-to-all-done), channel_id=1, source_target_pairs={{0,8},{8,0},{1,9},{9,1},{2,10},{10,2},{3,11},{11,3},{4,12},{12,4},... | collective-permute-start | bytes 1720328 | tf_op jit(solution)/shard_map/ppermute | solution.py:47
  52.8 2.2 %copy-start = (bf16[4,2,80,896]{3,2,1,0:T(8,128)(2,1)}, bf16[4,2,80,896]{3,2,1,0:T(8,128)(2,1)S(1)}, u32[]{:S(2)}) copy-start(bf16[4,2,80,896]{3,2,1,0:T(8,128)(2,1)S(1)} %pad_maximum_fusion) | copy-start | bytes 3440644
  55.0 3.0 %copy-start.4 = (bf16[384,896]{1,0:T(8,128)(2,1)S(1)}, bf16[384,896]{1,0:T(8,128)(2,1)}, u32[]{:S(2)}) copy-start(bf16[384,896]{1,0:T(8,128)(2,1)} %convolution_convert_fusion.3) | copy-start | bytes 2064388
  94.3 20.2 %all-to-all-start.2 = ((bf16[8,48,1920]{2,1,0:T(8,128)(2,1)}), bf16[8,48,1920]{2,1,0:T(8,128)(2,1)}, u32[]{:S(2)}, u32[]{:S(2)}) async-start(bf16[8,48,1920]{2,1,0:T(8,128)(2,1)} %broadcast_in_dim.10), calls=%async_computation.2 | async-start | bytes 2949120 | tf_op jit(solution)/shard_map/all_to_all | solution.py:19
  98.6 18.8 %copy-start.1 = (bf16[4,2,80,896]{3,2,1,0:T(8,128)(2,1)S(1)}, bf16[4,2,80,896]{3,2,1,0:T(8,128)(2,1)}, u32[]{:S(2)}) copy-start(bf16[4,2,80,896]{3,2,1,0:T(8,128)(2,1)} %copy-done) | copy-start | bytes 3440644
  119.5 1.2 copy-start.3
  125.7 24.3 %collective-permute-start.1 = (bf16[4,1120,128]{2,1,0:T(8,128)(2,1)S(1)}, bf16[4,1120,128]{2,1,0:T(8,128)(2,1)}, u32[]{:S(2)}, u32[]{:S(2)}) collective-permute-start(bf16[4,1120,128]{2,1,0:T(8,128)(2,1)S(1)} %select_bitcast_fusion), channel_id=1, source_target_pairs={{0,8},{8,0},{1,9},{9,1},{2,10},{10,2},{3,11},{11,3},{4,12},{12,4},... | collective-permute-start | bytes 3440648 | tf_op jit(solution)/shard_map/ppermute | solution.py:47
  145.6 31.2 %all-to-all-start.3 = ((bf16[8,56,768]{2,1,0:T(8,128)(2,1)}), bf16[8,56,768]{2,1,0:T(8,128)(2,1)}, u32[]{:S(2)}, u32[]{:S(2)}) async-start(bf16[8,56,768]{2,1,0:T(8,128)(2,1)} %pad_maximum_fusion.1), calls=%async_computation.3 | async-start | bytes 1376256 | tf_op jit(solution)/shard_map/all_to_all | solution.py:19
  151.8 52.7 %collective-permute-start.2 = (bf16[1120,128]{1,0:T(8,128)(2,1)S(1)}, bf16[1120,128]{1,0:T(8,128)(2,1)S(1)}, u32[]{:S(2)}, u32[]{:S(2)}) collective-permute-start(bf16[1120,128]{1,0:T(8,128)(2,1)S(1)} %get-tuple-element.29), channel_id=1, source_target_pairs={{0,16},{16,0},{32,48},{48,32},{1,17},{17,1},{33,49},{49,33},{2,18}... | collective-permute-start | bytes 860168 | tf_op jit(solution)/shard_map/ppermute | solution.py:47
  171.8 32.7 %collective-permute-start.4 = (bf16[1120,128]{1,0:T(8,128)(2,1)S(1)}, bf16[1120,128]{1,0:T(8,128)(2,1)S(1)}, u32[]{:S(2)}, u32[]{:S(2)}) collective-permute-start(bf16[1120,128]{1,0:T(8,128)(2,1)S(1)} %get-tuple-element.30), channel_id=1, source_target_pairs={{0,48},{16,32},{32,16},{48,0},{1,49},{17,33},{33,17},{49,1},{2,50}... | collective-permute-start | bytes 860168 | tf_op jit(solution)/shard_map/ppermute | solution.py:47
  173.8 30.7 %collective-permute-start.3 = (bf16[1120,128]{1,0:T(8,128)(2,1)S(1)}, bf16[1120,128]{1,0:T(8,128)(2,1)S(1)}, u32[]{:S(2)}, u32[]{:S(2)}) collective-permute-start(bf16[1120,128]{1,0:T(8,128)(2,1)S(1)} %get-tuple-element.31), channel_id=1, source_target_pairs={{0,32},{16,48},{32,0},{48,16},{1,33},{17,49},{33,1},{49,17},{2,34}... | collective-permute-start | bytes 860168 | tf_op jit(solution)/shard_map/ppermute | solution.py:47
  177.7 15.7 %collective-permute-start.5 = (f32[640]{0:T(1024)S(1)}, f32[640]{0:T(1024)S(1)}, u32[]{:S(2)}, u32[]{:S(2)}) collective-permute-start(f32[640]{0:T(1024)S(1)} %convert_reduce_fusion.8), channel_id=1, source_target_pairs={{0,16},{16,0},{32,48},{48,32},{1,17},{17,1},{33,49},{49,33},{2,18}... | collective-permute-start | bytes 7688 | tf_op jit(solution)/shard_map/ppermute | solution.py:47
  193.5 6.6 %collective-permute-start.6 = (f32[640]{0:T(1024)S(1)}, f32[640]{0:T(1024)S(1)}, u32[]{:S(2)}, u32[]{:S(2)}) collective-permute-start(f32[640]{0:T(1024)S(1)} %add.288), channel_id=1, source_target_pairs={{0,32},{16,48},{32,0},{48,16},{1,33},{17,49},{33,1},{49,17},{2,34}... | collective-permute-start | bytes 7688 | tf_op jit(solution)/shard_map/ppermute | solution.py:47
  200.1 3.8 %collective-permute-start.7 = (f32[640]{0:T(1024)S(1)}, f32[640]{0:T(1024)S(1)}, u32[]{:S(2)}, u32[]{:S(2)}) collective-permute-start(f32[640]{0:T(1024)S(1)} %add.289), channel_id=1, source_target_pairs={{0,8},{8,0},{1,9},{9,1},{2,10},{10,2},{3,11},{11,3},{4,12},{12,4},... | collective-permute-start | bytes 7688 | tf_op jit(solution)/shard_map/ppermute | solution.py:47
  204.8 0.7 copy-start.9
  205.5 0.7 copy-start.8
Sparse Core Ops, SparseCore 0:
  10.1 43.4 all-gather.1
where the time goes:
time: 214 us; the launch traced here: 213 us
  starting transfers between devices  86.4 us (40%)
  blocking collectives  59.3 us (28%)
  waiting for transfers between devices  20.4 us (10%)
  between operations  14.7 us (7%)
  matrix products  11 us (5%)
  other arithmetic  10.9 us (5%)
  local copies, waits for them, and re-layouts  10.2 us (5%)
    ppermute x8, starting transfers between devices, swap(): lax.ppermute(value, axis, [(i, i ^ bits) for i in range(lax.axis_size(axi...  72.5 us
    all_to_all x1, blocking collectives, exchange(): return lax.all_to_all(blocks, axis, 0, 0, tiled=True)  31.1 us
    all_gather x1, blocking collectives, body(): lax.all_gather(jnp.concatenate([x_in, d_out], axis=1), 'gx', axis=0, tile...  28.2 us
    all_to_all x3, waiting for transfers between devices, exchange(): return lax.all_to_all(blocks, axis, 0, 0, tiled=True)  15.7 us
    all_to_all x3, starting transfers between devices, exchange(): return lax.all_to_all(blocks, axis, 0, 0, tiled=True)  13.9 us
    dot_general x6, matrix products, dot(): lax.dot_general(a, b, ((contract[:1], contract[1:]), ((), ())), preferred...  11 us
  transfers between devices with their start and end apart: 12, of which 4 were waited for; matrix products, arithmetic and copies ran while one was open for 5% of the time, Pallas kernels for 0%

commit v1 on v0

--- a/solution.py
+++ b/solution.py
@@ -7,6 +7,11 @@
 BF, F32 = (jnp.bfloat16, jnp.float32)
 LANES = 128
 GY, GZ = (("yl", "co"), ("yh", "xx"))
+
+
+def gather_over(shard, mesh_axis, d):
+    repeated = jnp.stack([shard] * lax.axis_size(mesh_axis))
+    return jnp.concatenate(lax.all_to_all(repeated, mesh_axis, 0, 0), axis=d)
 
 
 def gelu_pair(hidden):
@@ -73,7 +78,7 @@
 
     down_full = lax.all_gather(w_down, GY, axis=0, tiled=True)
     up_mine = spread(w_up, "yl")
-    both = lax.all_gather(jnp.concatenate([x_in, d_out], axis=1), "gx", axis=0, tiled=True)
+    both = gather_over(jnp.concatenate([x_in, d_out], axis=1), "gx", 0)
     both, up_mine = lax.optimization_barrier((both, up_mine))
     up_full = by_core(up_mine, other_core(up_mine))
     x_rows, out_rows = (both[:, :local].astype(F32), both[:, local:])

time: 214 us -> 240 us (1.12)
  waiting for transfers between devices: 20.4 us -> 91.1 us
  starting transfers between devices: 86.4 us -> 56 us
  blocking collectives: 59.3 us -> 43 us
    ppermute x8, starting transfers between devices: 72.5 us -> 24.2 us  [swap(): lax.ppermute(value, axis, [(i, i ^ bits) for i in range(lax.axis_size(axi...]
    all_to_all x3, waiting for transfers between devices: 15.7 us -> 48.1 us  [exchange(): return lax.all_to_all(blocks, axis, 0, 0, tiled=True)]
    all_gather x1 -> x0, blocking collectives: 28.2 us -> none  [body(): lax.all_gather(jnp.concatenate([x_in, d_out], axis=1), 'gx', axis=0, tile...]
    all_to_all x0 -> x1, waiting for transfers between devices: none -> 27 us  [gather_over(): return jnp.concatenate(lax.all_to_all(repeated, mesh_axis, 0, 0), axis=d)]
    all_to_all x0 -> x1, starting transfers between devices: none -> 13.4 us  [gather_over(): return jnp.concatenate(lax.all_to_all(repeated, mesh_axis, 0, 0), axis=d)]
    all_to_all x1, blocking collectives: 31.1 us -> 43 us  [exchange(): return lax.all_to_all(blocks, axis, 0, 0, tiled=True)]
    all_gather x1, waiting for transfers between devices: 0.01 us -> 11.4 us  [body(): down_full = lax.all_gather(w_down, GY, axis=0, tiled=True)]
    all_to_all x3, starting transfers between devices: 13.9 us -> 18.4 us  [exchange(): return lax.all_to_all(blocks, axis, 0, 0, tiled=True)]
  transfers between devices with their start and end apart: 12 -> 13, of which waited for: 4 -> 8; matrix products, arithmetic and copies ran while one was open for 5% -> 4% of each run, Pallas kernels for 0% -> 0%
where the time goes in v1:
time: 240 us; the launch traced here: 239 us
  waiting for transfers between devices  91.1 us (38%)
  starting transfers between devices  56 us (23%)
  blocking collectives  43 us (18%)
  between operations  14.6 us (6%)
  local copies, waits for them, and re-layouts  11.9 us (5%)
  other arithmetic  11.1 us (5%)
  matrix products  11 us (5%)
    all_to_all x3, waiting for transfers between devices, exchange(): return lax.all_to_all(blocks, axis, 0, 0, tiled=True)  48.1 us
    all_to_all x1, blocking collectives, exchange(): return lax.all_to_all(blocks, axis, 0, 0, tiled=True)  43 us
    all_to_all x1, waiting for transfers between devices, gather_over(): return jnp.concatenate(lax.all_to_all(repeated, mesh_axis, 0, 0), axis=d)  27 us
    ppermute x8, starting transfers between devices, swap(): lax.ppermute(value, axis, [(i, i ^ bits) for i in range(lax.axis_size(axi...  24.2 us
    all_to_all x3, starting transfers between devices, exchange(): return lax.all_to_all(blocks, axis, 0, 0, tiled=True)  18.4 us
    all_to_all x1, starting transfers between devices, gather_over(): return jnp.concatenate(lax.all_to_all(repeated, mesh_axis, 0, 0), axis=d)  13.4 us
    all_gather x1, waiting for transfers between devices, body(): down_full = lax.all_gather(w_down, GY, axis=0, tiled=True)  11.4 us
    dot_general x6, matrix products, dot(): lax.dot_general(a, b, ((contract[:1], contract[1:]), ((), ())), preferred...  11 us
  transfers between devices with their start and end apart: 13, of which 8 were waited for; matrix products, arithmetic and copies ran while one was open for 4% of the time, Pallas kernels for 0%

profile of v1, /device:TPU:1, one launch (start us, length us, event | category | flops | bytes accessed | tf_op | source)
XLA Modules:
  0.0 238.7 jit_solution(14245137097369560397)
XLA Ops:
  7.2 1.8 broadcast_in_dim.8
  9.0 5.4 %all-to-all-start.1 = ((bf16[4,80,896]{2,1,0:T(8,128)(2,1)}), bf16[4,80,896]{2,1,0:T(8,128)(2,1)S(1)}, u32[]{:S(2)}, u32[]{:S(2)}) async-start(bf16[4,80,896]{2,1,0:T(8,128)(2,1)} %broadcast_in_dim.8), calls=%async_computation.1 | async-start | bytes 1146880 | tf_op jit(solution)/shard_map/all_to_all | solution.py:24
  14.4 11.6 %all-to-all-done.1 = bf16[4,80,896]{2,1,0:T(8,128)(2,1)S(1)} async-done(((bf16[4,80,896]{2,1,0:T(8,128)(2,1)}), bf16[4,80,896]{2,1,0:T(8,128)(2,1)S(1)}, u32[]{:S(2)}, u32[]{:S(2)}) %all-to-all-start.1) | async-done | bytes 573472 | tf_op jit(solution)/shard_map/all_to_all | solution.py:24
  26.1 1.1 stack.26
  27.1 13.4 %all-to-all-start = ((bf16[8,48,1280]{2,1,0:T(8,128)(2,1)}), bf16[8,48,1280]{2,1,0:T(8,128)(2,1)S(1)}, u32[]{:S(2)}, u32[]{:S(2)}) async-start(bf16[8,48,1280]{2,1,0:T(8,128)(2,1)} %stack.26), calls=%async_computation | async-start | bytes 1966080 | tf_op jit(solution)/shard_map/all_to_all | solution.py:14
  40.6 0.7 all-gather.2.cloned.1.call-update
  41.4 27.0 %all-to-all-done = bf16[8,48,1280]{2,1,0:T(8,128)(2,1)S(1)} async-done(((bf16[8,48,1280]{2,1,0:T(8,128)(2,1)}), bf16[8,48,1280]{2,1,0:T(8,128)(2,1)S(1)}, u32[]{:S(2)}, u32[]{:S(2)}) %all-to-all-start) | async-done | bytes 983072 | tf_op jit(solution)/shard_map/all_to_all | solution.py:14
  68.3 2.4 %collective-permute-start = (bf16[4,80,896]{2,1,0:T(8,128)(2,1)S(1)}, bf16[4,80,896]{2,1,0:T(8,128)(2,1)S(1)}, u32[]{:S(2)}, u32[]{:S(2)}) collective-permute-start(bf16[4,80,896]{2,1,0:T(8,128)(2,1)S(1)} %all-to-all-done.1), channel_id=1, source_target_pairs={{0,8},{8,0},{1,9},{9,1},{2,10},{10,2},{3,11},{11,3},{4,12},{12,4},... | collective-permute-start | bytes 1720328 | tf_op jit(solution)/shard_map/ppermute | solution.py:52
  70.7 0.1 convert_reduce_fusion
  70.9 0.3 fusion.5
  71.2 0.2 copy.145
  71.5 11.4 %all-gather.2.cloned.1.call-done = bf16[896,640]{1,0:T(8,128)(2,1)} async-done(((bf16[112,640]{1,0:T(8,128)(2,1)}), bf16[896,640]{1,0:T(8,128)(2,1)}) %all-gather.2.cloned.1.call-update) | async-done | bytes 1146896 | tf_op jit(solution)/shard_map/all_gather | solution.py:79
  82.8 2.9 %convolution_convert_fusion.2 = bf16[384,896]{1,0:T(8,128)(2,1)} fusion(bf16[896,640]{1,0:T(8,128)(2,1)} %all-gather.2.cloned.1.call-done, bf16[384,1280]{1,0:T(8,128)(2,1)S(1)} %bitcast.160), kind=kOutput, calls=%fused_computation.10 | convolution fusion | flops 440745984 | bytes 2326528 | tf_op jit(solution)/shard_map/dot_general | solution.py:60
  85.8 0.1 select_bitcast_fusion.2
  85.9 0.1 pad_maximum_fusion
  86.0 1.7 convolution_convert_fusion.3
  87.7 0.3 convolution_reduce_fusion
  88.0 0.1 reshape.510
  88.2 0.7 copy-done.4
  88.8 2.1 concatenate.25
  90.9 43.0 %all_to_all.25 = bf16[8,48,1920]{2,1,0:T(8,128)(2,1)S(1)} all-to-all(bf16[8,48,1920]{2,1,0:T(8,128)(2,1)S(1)} %concatenate.25), channel_id=1, replica_groups=mesh['gx'=8,'yl'=4,'co'=2,'yh'=2,'xx'=4] {'yh','xx'}, dimensions={0} | all-to-all | bytes 2949120 | tf_op jit(solution)/shard_map/all_to_all | solution.py:24
  134.0 0.2 convert_reduce_fusion.6
  134.3 0.1 fusion.35
  135.0 0.2 convert_reduce_fusion.1
  135.2 0.2 multiply_convert_fusion
  135.4 0.2 multiply_reduce_fusion.1
  135.7 0.1 copy.146
  135.8 1.2 broadcast_in_dim.10
  137.0 6.2 %all-to-all-start.3 = ((bf16[8,48,1920]{2,1,0:T(8,128)(2,1)}), bf16[8,48,1920]{2,1,0:T(8,128)(2,1)}, u32[]{:S(2)}, u32[]{:S(2)}) async-start(bf16[8,48,1920]{2,1,0:T(8,128)(2,1)} %broadcast_in_dim.10), calls=%async_computation.3 | async-start | bytes 2949120 | tf_op jit(solution)/shard_map/all_to_all | solution.py:24
  143.2 0.1 convert_reduce_fusion.7
  143.4 25.3 %all-to-all-done.3 = bf16[8,48,1920]{2,1,0:T(8,128)(2,1)} async-done(((bf16[8,48,1920]{2,1,0:T(8,128)(2,1)}), bf16[8,48,1920]{2,1,0:T(8,128)(2,1)}, u32[]{:S(2)}, u32[]{:S(2)}) %all-to-all-start.3) | async-done | bytes 1474592 | tf_op jit(solution)/shard_map/all_to_all | solution.py:24
  168.7 1.2 fusion.108
  169.9 1.3 multiply_reduce_fusion
  171.2 0.1 copy.141
  171.3 0.1 copy.140
  171.5 0.1 copy.142
  171.6 2.1 fusion.111
  173.8 0.2 copy.120
  174.0 0.9 pad_maximum_fusion.1
  175.0 2.1 convolution_convert_fusion
  177.0 2.0 convolution_convert_fusion.1
  179.0 0.2 fusion.109
  179.2 0.2 fusion.110
  179.8 0.1 select_bitcast_fusion
  179.9 5.3 %collective-permute-start.1 = (bf16[4,1120,128]{2,1,0:T(8,128)(2,1)S(1)}, bf16[4,1120,128]{2,1,0:T(8,128)(2,1)}, u32[]{:S(2)}, u32[]{:S(2)}) collective-permute-start(bf16[4,1120,128]{2,1,0:T(8,128)(2,1)S(1)} %select_bitcast_fusion), channel_id=1, source_target_pairs={{0,8},{8,0},{1,9},{9,1},{2,10},{10,2},{3,11},{11,3},{4,12},{12,4},... | collective-permute-start | bytes 3440648 | tf_op jit(solution)/shard_map/ppermute | solution.py:52
  185.3 6.8 %all-to-all-start.4 = ((bf16[8,56,768]{2,1,0:T(8,128)(2,1)}), bf16[8,56,768]{2,1,0:T(8,128)(2,1)}, u32[]{:S(2)}, u32[]{:S(2)}) async-start(bf16[8,56,768]{2,1,0:T(8,128)(2,1)} %pad_maximum_fusion.1), calls=%async_computation.4 | async-start | bytes 1376256 | tf_op jit(solution)/shard_map/all_to_all | solution.py:24
  192.2 1.8 fusion
  194.1 1.9 collective-permute-start.2
  196.0 3.7 %collective-permute-start.4 = (bf16[1120,128]{1,0:T(8,128)(2,1)S(1)}, bf16[1120,128]{1,0:T(8,128)(2,1)S(1)}, u32[]{:S(2)}, u32[]{:S(2)}) collective-permute-start(bf16[1120,128]{1,0:T(8,128)(2,1)S(1)} %get-tuple-element.30), channel_id=1, source_target_pairs={{0,48},{16,32},{32,16},{48,0},{1,49},{17,33},{33,17},{49,1},{2,50}... | collective-permute-start | bytes 860168 | tf_op jit(solution)/shard_map/ppermute | solution.py:52
  199.7 2.8 %collective-permute-start.3 = (bf16[1120,128]{1,0:T(8,128)(2,1)S(1)}, bf16[1120,128]{1,0:T(8,128)(2,1)S(1)}, u32[]{:S(2)}, u32[]{:S(2)}) collective-permute-start(bf16[1120,128]{1,0:T(8,128)(2,1)S(1)} %get-tuple-element.31), channel_id=1, source_target_pairs={{0,32},{16,48},{32,0},{48,16},{1,33},{17,49},{33,1},{49,17},{2,34}... | collective-permute-start | bytes 860168 | tf_op jit(solution)/shard_map/ppermute | solution.py:52
  202.5 11.2 %all-to-all-done.4 = bf16[8,56,768]{2,1,0:T(8,128)(2,1)} async-done(((bf16[8,56,768]{2,1,0:T(8,128)(2,1)}), bf16[8,56,768]{2,1,0:T(8,128)(2,1)}, u32[]{:S(2)}, u32[]{:S(2)}) %all-to-all-start.4) | async-done | bytes 688160 | tf_op jit(solution)/shard_map/all_to_all | solution.py:24
  213.7 0.9 convert_reduce_fusion.8
  214.6 1.9 collective-permute-start.5
  216.5 0.9 convert_reduce_fusion.4
  217.4 0.2 slice_reduce_fusion.1
  217.6 1.3 collective-permute-done.5
  218.9 2.8 %collective-permute-start.6 = (f32[640]{0:T(1024)S(1)}, f32[640]{0:T(1024)S(1)}, u32[]{:S(2)}, u32[]{:S(2)}) collective-permute-start(f32[640]{0:T(1024)S(1)} %add.288), channel_id=1, source_target_pairs={{0,32},{16,48},{32,0},{48,16},{1,33},{17,49},{33,1},{49,17},{2,34}... | collective-permute-start | bytes 7688 | tf_op jit(solution)/shard_map/ppermute | solution.py:52
  221.7 1.1 convert_reduce_fusion.3
  222.8 2.6 %collective-permute-done.6 = f32[640]{0:T(1024)S(1)} collective-permute-done((f32[640]{0:T(1024)S(1)}, f32[640]{0:T(1024)S(1)}, u32[]{:S(2)}, u32[]{:S(2)}) %collective-permute-start.6) | collective-permute-done | bytes 2592 | tf_op jit(solution)/shard_map/ppermute | solution.py:52
  225.5 3.4 %collective-permute-start.7 = (f32[640]{0:T(1024)S(1)}, f32[640]{0:T(1024)S(1)}, u32[]{:S(2)}, u32[]{:S(2)}) collective-permute-start(f32[640]{0:T(1024)S(1)} %add.289), channel_id=1, source_target_pairs={{0,8},{8,0},{1,9},{9,1},{2,10},{10,2},{3,11},{11,3},{4,12},{12,4},... | collective-permute-start | bytes 7688 | tf_op jit(solution)/shard_map/ppermute | solution.py:52
  228.9 0.7 multiply_convert_fusion.1
  229.7 0.6 add.290
  230.7 0.5 copy-done.9
  231.2 0.7 copy-done.8
  (99 shorter events, 2.4 us)
Async XLA Ops:
  7.2 7.2 %copy-start.5 = (bf16[48,640]{1,0:T(8,128)(2,1)S(1)}, bf16[48,640]{1,0:T(8,128)(2,1)}, u32[]{:S(2)}) copy-start(bf16[48,640]{1,0:T(8,128)(2,1)} %param.5) | copy-start | bytes 184324
  7.2 7.2 %copy-start.6 = (bf16[48,640]{1,0:T(8,128)(2,1)S(1)}, bf16[48,640]{1,0:T(8,128)(2,1)}, u32[]{:S(2)}) copy-start(bf16[48,640]{1,0:T(8,128)(2,1)} %param.9) | copy-start | bytes 184324
  9.0 17.1 %all-to-all-start.1 = ((bf16[4,80,896]{2,1,0:T(8,128)(2,1)}), bf16[4,80,896]{2,1,0:T(8,128)(2,1)S(1)}, u32[]{:S(2)}, u32[]{:S(2)}) async-start(bf16[4,80,896]{2,1,0:T(8,128)(2,1)} %broadcast_in_dim.8), calls=%async_computation.1 | async-start | bytes 1146880 | tf_op jit(solution)/shard_map/all_to_all | solution.py:24
  14.4 26.9 %copy-start.7 = (f32[640]{0:T(1024)S(1)}, f32[640]{0:T(1024)}, u32[]{:S(2)}) copy-start(f32[640]{0:T(1024)} %param.6) | copy-start | bytes 7684
  27.1 41.2 %all-to-all-start = ((bf16[8,48,1280]{2,1,0:T(8,128)(2,1)}), bf16[8,48,1280]{2,1,0:T(8,128)(2,1)S(1)}, u32[]{:S(2)}, u32[]{:S(2)}) async-start(bf16[8,48,1280]{2,1,0:T(8,128)(2,1)} %stack.26), calls=%async_computation | async-start | bytes 1966080 | tf_op jit(solution)/shard_map/all_to_all | solution.py:14
  40.5 42.3 %all-gather.2.cloned.1.call-start = ((), (), s32[]{:S(2)}) async-start(), calls=%async_computation.5 | async-start | bytes 1290240 | tf_op jit(solution)/shard_map/all_gather | solution.py:79
  68.3 17.7 %copy-start.2 = (bf16[8,48,1280]{2,1,0:T(8,128)(2,1)}, bf16[8,48,1280]{2,1,0:T(8,128)(2,1)S(1)}, u32[]{:S(2)}) copy-start(bf16[8,48,1280]{2,1,0:T(8,128)(2,1)S(1)} %all-to-all-done) | copy-start | bytes 2949124
  68.3 17.4 %collective-permute-start = (bf16[4,80,896]{2,1,0:T(8,128)(2,1)S(1)}, bf16[4,80,896]{2,1,0:T(8,128)(2,1)S(1)}, u32[]{:S(2)}, u32[]{:S(2)}) collective-permute-start(bf16[4,80,896]{2,1,0:T(8,128)(2,1)S(1)} %all-to-all-done.1), channel_id=1, source_target_pairs={{0,8},{8,0},{1,9},{9,1},{2,10},{10,2},{3,11},{11,3},{4,12},{12,4},... | collective-permute-start | bytes 1720328 | tf_op jit(solution)/shard_map/ppermute | solution.py:52
  86.0 1.7 copy-start
  87.7 1.1 copy-start.4
  137.0 31.6 %all-to-all-start.3 = ((bf16[8,48,1920]{2,1,0:T(8,128)(2,1)}), bf16[8,48,1920]{2,1,0:T(8,128)(2,1)}, u32[]{:S(2)}, u32[]{:S(2)}) async-start(bf16[8,48,1920]{2,1,0:T(8,128)(2,1)} %broadcast_in_dim.10), calls=%async_computation.3 | async-start | bytes 2949120 | tf_op jit(solution)/shard_map/all_to_all | solution.py:24
  143.2 28.4 %copy-start.1 = (bf16[4,2,80,896]{3,2,1,0:T(8,128)(2,1)S(1)}, bf16[4,2,80,896]{3,2,1,0:T(8,128)(2,1)}, u32[]{:S(2)}) copy-start(bf16[4,2,80,896]{3,2,1,0:T(8,128)(2,1)} %copy-done) | copy-start | bytes 3440644
  173.8 1.2 copy-start.3
  179.9 12.3 %collective-permute-start.1 = (bf16[4,1120,128]{2,1,0:T(8,128)(2,1)S(1)}, bf16[4,1120,128]{2,1,0:T(8,128)(2,1)}, u32[]{:S(2)}, u32[]{:S(2)}) collective-permute-start(bf16[4,1120,128]{2,1,0:T(8,128)(2,1)S(1)} %select_bitcast_fusion), channel_id=1, source_target_pairs={{0,8},{8,0},{1,9},{9,1},{2,10},{10,2},{3,11},{11,3},{4,12},{12,4},... | collective-permute-start | bytes 3440648 | tf_op jit(solution)/shard_map/ppermute | solution.py:52
  185.3 28.4 %all-to-all-start.4 = ((bf16[8,56,768]{2,1,0:T(8,128)(2,1)}), bf16[8,56,768]{2,1,0:T(8,128)(2,1)}, u32[]{:S(2)}, u32[]{:S(2)}) async-start(bf16[8,56,768]{2,1,0:T(8,128)(2,1)} %pad_maximum_fusion.1), calls=%async_computation.4 | async-start | bytes 1376256 | tf_op jit(solution)/shard_map/all_to_all | solution.py:24
  194.1 36.2 %collective-permute-start.2 = (bf16[1120,128]{1,0:T(8,128)(2,1)S(1)}, bf16[1120,128]{1,0:T(8,128)(2,1)S(1)}, u32[]{:S(2)}, u32[]{:S(2)}) collective-permute-start(bf16[1120,128]{1,0:T(8,128)(2,1)S(1)} %get-tuple-element.29), channel_id=1, source_target_pairs={{0,16},{16,0},{32,48},{48,32},{1,17},{17,1},{33,49},{49,33},{2,18}... | collective-permute-start | bytes 860168 | tf_op jit(solution)/shard_map/ppermute | solution.py:52
  196.0 34.3 %collective-permute-start.4 = (bf16[1120,128]{1,0:T(8,128)(2,1)S(1)}, bf16[1120,128]{1,0:T(8,128)(2,1)S(1)}, u32[]{:S(2)}, u32[]{:S(2)}) collective-permute-start(bf16[1120,128]{1,0:T(8,128)(2,1)S(1)} %get-tuple-element.30), channel_id=1, source_target_pairs={{0,48},{16,32},{32,16},{48,0},{1,49},{17,33},{33,17},{49,1},{2,50}... | collective-permute-start | bytes 860168 | tf_op jit(solution)/shard_map/ppermute | solution.py:52
  199.7 30.6 %collective-permute-start.3 = (bf16[1120,128]{1,0:T(8,128)(2,1)S(1)}, bf16[1120,128]{1,0:T(8,128)(2,1)S(1)}, u32[]{:S(2)}, u32[]{:S(2)}) collective-permute-start(bf16[1120,128]{1,0:T(8,128)(2,1)S(1)} %get-tuple-element.31), channel_id=1, source_target_pairs={{0,32},{16,48},{32,0},{48,16},{1,33},{17,49},{33,1},{49,17},{2,34}... | collective-permute-start | bytes 860168 | tf_op jit(solution)/shard_map/ppermute | solution.py:52
  214.6 4.4 %collective-permute-start.5 = (f32[640]{0:T(1024)S(1)}, f32[640]{0:T(1024)S(1)}, u32[]{:S(2)}, u32[]{:S(2)}) collective-permute-start(f32[640]{0:T(1024)S(1)} %convert_reduce_fusion.8), channel_id=1, source_target_pairs={{0,16},{16,0},{32,48},{48,32},{1,17},{17,1},{33,49},{49,33},{2,18}... | collective-permute-start | bytes 7688 | tf_op jit(solution)/shard_map/ppermute | solution.py:52
  218.9 6.5 %collective-permute-start.6 = (f32[640]{0:T(1024)S(1)}, f32[640]{0:T(1024)S(1)}, u32[]{:S(2)}, u32[]{:S(2)}) collective-permute-start(f32[640]{0:T(1024)S(1)} %add.288), channel_id=1, source_target_pairs={{0,32},{16,48},{32,0},{48,16},{1,33},{17,49},{33,1},{49,17},{2,34}... | collective-permute-start | bytes 7688 | tf_op jit(solution)/shard_map/ppermute | solution.py:52
  225.5 4.2 %collective-permute-start.7 = (f32[640]{0:T(1024)S(1)}, f32[640]{0:T(1024)S(1)}, u32[]{:S(2)}, u32[]{:S(2)}) collective-permute-start(f32[640]{0:T(1024)S(1)} %add.289), channel_id=1, source_target_pairs={{0,8},{8,0},{1,9},{9,1},{2,10},{10,2},{3,11},{11,3},{4,12},{12,4},... | collective-permute-start | bytes 7688 | tf_op jit(solution)/shard_map/ppermute | solution.py:52
  230.6 0.7 copy-start.9
  231.2 0.7 copy-start.8
Sparse Core Ops, SparseCore 0:
  43.5 39.3 all-gather.1
